TPU v7x, 256 devices: a whole 4x4x8 slice. The times are simulated.
256 devices in a mesh: samp: 64 (over z, y, core), var: 4 (over x).
Axes of the slice: x: 4, y: 4, z: 8, core: 2. Of those that a mesh axis runs over, the one named last changes fastest.
Arguments:
- dosage: bfloat16 [16384, 40960], P('samp', 'var'), may hold values from 0 to 2
- centers: float32 [40960], replicated, may hold values from 0.4 to 1.34
- scales: float32 [40960], replicated, may hold values from 1.6 to 2.2
- phenotype: float32 [16384], P('samp'), may hold values from -6 to 6
- fold_ids: int32 [16384], P('samp'), may hold values from 0 to 3
- strong_blocks: int32 [32], replicated, may hold values from 0 to 319, as said below
- warm_start: float32 [4096, 32], replicated, may hold values from -4 to 4
- penalty: float32 [8], replicated, may hold values from 0.05 to 0.5
- step_size: float32 [32], replicated, may hold values from 0.2 to 0.6
Outputs:
- margin: float32 [40960], P('var')
- coefficients: float32 [4096, 32], P('var')
Inputs may be any that keep to these rules, and one draw needn't show every extreme that they name: `strong_blocks`: 32 different block numbers.
All inputs are finite; a program needn't handle non-finite values.
Results may differ from a plain program's by a relative error of at most 0.0075.
Values may be sent and summed in bfloat16 or wider, within the bound.
No kernel may reach another device: no remote copies, remote signals or barrier semaphores. Data moves between devices by JAX's collectives and lax.ppermute only.
A program may use at most 64 MiB of HBM per device.

v0:
```python
import math
import jax
import jax.numpy as jnp
from jax import lax
from jax.sharding import PartitionSpec as P

BLOCK = 128
NS = 4096
LAMBDAS = 8
FOLDS = 4
ITERS = 3
exact_mode = lax.Precision.HIGHEST


def shards(
    dosage, centers, scales, phenotype, fold_ids, strong_blocks, warm_start, penalty, step_size
):
    rows, local_width = dosage.shape
    groups = lax.axis_size("var")
    place = lax.axis_index("var")
    fit_total = LAMBDAS * FOLDS
    fit_folds = jnp.arange(fit_total, dtype=jnp.int32) % FOLDS
    weights = (fold_ids[:, None] != fit_folds[None, :]).astype(jnp.float32)
    counts = lax.psum(jnp.sum(weights, axis=0), "samp")
    fit_penalty = jnp.repeat(penalty, FOLDS)
    threshold = step_size * fit_penalty
    local_blocks = local_width // BLOCK
    relative = strong_blocks - place * local_blocks
    owned = (relative >= 0) & (relative < local_blocks)
    picked = jnp.take(
        dosage.reshape(rows, local_blocks, BLOCK), jnp.clip(relative, 0, local_blocks - 1), axis=1
    )
    masked = (picked * owned.astype(jnp.bfloat16)[None, :, None]).reshape(rows, NS)
    columns = (
        strong_blocks[:, None] * BLOCK + jnp.arange(BLOCK, dtype=jnp.int32)[None, :]
    ).reshape(NS)
    strong_centers = centers[columns]
    strong_scales = scales[columns]
    owned_columns = jnp.repeat(owned.astype(jnp.float32), BLOCK)
    share = NS // groups
    point = warm_start
    part_centers = strong_centers * owned_columns
    part_threshold = threshold[None, :]

    def residual_of(coef):
        scaled = (strong_scales[:, None] * coef).astype(jnp.bfloat16)
        partial_fit = jnp.dot(masked, scaled, preferred_element_type=jnp.float32)
        partial_fit = (
            partial_fit - jnp.dot(part_centers * strong_scales, coef, precision=exact_mode)[None, :]
        )
        fitted = lax.psum(partial_fit.astype(jnp.bfloat16), "var").astype(jnp.float32)
        return (weights * (phenotype[:, None] - fitted)).astype(jnp.bfloat16)

    rounded = residual_of(point)
    column_sums = jnp.sum(rounded.astype(jnp.float32), axis=0)
    local_centers = lax.dynamic_slice_in_dim(centers, place * local_width, local_width, 0)
    local_scales = lax.dynamic_slice_in_dim(scales, place * local_width, local_width, 0)
    cross = lax.dot_general(
        dosage, rounded, (((0,), (0,)), ((), ())), preferred_element_type=jnp.float32
    )
    total = lax.psum(cross - local_centers[:, None] * column_sums[None, :], "samp")
    margin = jnp.max(
        jnp.abs(local_scales[:, None] * total / counts[None, :]) / fit_penalty[None, :], axis=1
    )
    momentum = 1.0
    previous = point
    for sweep in range(ITERS):
        if sweep > 0:
            rounded = residual_of(point)
            column_sums = jnp.sum(rounded.astype(jnp.float32), axis=0)
        gradient_cross = lax.dot_general(
            masked, rounded, (((0,), (0,)), ((), ())), preferred_element_type=jnp.float32
        )
        gradient_cross = gradient_cross - part_centers[:, None] * column_sums[None, :]
        gradient_total = lax.psum(gradient_cross, ("samp", "var"))
        moved = point + step_size[None, :] * (
            strong_scales[:, None] * gradient_total / counts[None, :]
        )
        current = moved - jnp.clip(moved, -part_threshold, part_threshold)
        following = (1.0 + math.sqrt(1.0 + 4.0 * momentum * momentum)) / 2.0
        point = current + (momentum - 1.0) / following * (current - previous)
        previous = current
        momentum = following
    coefficients = lax.dynamic_slice_in_dim(previous, place * share, share, 0)
    return (margin, coefficients)


def solution(mesh):
    return jax.shard_map(
        shards,
        mesh=mesh,
        in_specs=(P("samp", "var"), P(), P(), P("samp"), P("samp"), P(), P(), P(), P()),
        out_specs=(P("var"), P("var", None)),
        check_vma=False,
    )
```

profile of v0, /device:TPU:2, one launch (start us, length us, event | category | flops | bytes accessed | tf_op | source)
XLA Modules:
  0.0 1087.9 jit_solution(17105678928884932665)
XLA Ops:
  7.2 0.0 all-reduce.7.cloned.1.call-start
  7.2 7.9 copy.11
  15.2 7.9 copy.12
  23.1 3.4 gather_fusion
  26.6 2.9 copy.13
  29.5 0.1 broadcast_bitcast_fusion
  29.6 0.1 broadcast_bitcast_fusion.1
  29.7 0.1 iota_add_fusion
  29.8 23.0 %gather_fusion.1 = f32[4096]{0:T(1024)S(1)} fusion(f32[40960]{0:T(1024)S(1)} %copy-done.1, s32[4096]{0:T(1024)S(1)} %broadcast_clamp_fusion), kind=kCustom, calls=%fused_computation.1 | custom fusion | bytes 49152 | tf_op jit(solution)/shard_map/gather | solution.py:38
  52.9 23.0 %gather_fusion.2 = f32[4096]{0:T(1024)S(1)} fusion(f32[40960]{0:T(1024)S(1)} %copy-done, s32[4096]{0:T(1024)S(1)} %broadcast_clamp_fusion), kind=kCustom, calls=%fused_computation.2 | custom fusion | bytes 49152 | tf_op jit(solution)/shard_map/gather | solution.py:37
  75.9 0.1 fusion.23
  76.0 0.5 convolution_bitcast_fusion.3
  76.5 3.2 fusion.1
  79.7 0.4 fusion.3
  80.2 15.3 %psum.56 = bf16[256,32]{0,1:T(8,128)(2,1)S(1)} all-reduce(bf16[256,32]{0,1:T(8,128)(2,1)S(1)} %fusion.3), channel_id=1, replica_groups=mesh['samp'=64,'var'=4] {'var'}, use_global_device_ids=true, to_apply=%region_0.1 | all-reduce | flops 8192 | bytes 32768 | tf_op jit(solution)/shard_map/psum | solution.py:51
  95.5 0.2 fusion.11
  95.7 1.5 convolution_subtract_fusion.2
  97.2 0.0 all-reduce.7.cloned.1.call-update
  97.2 0.0 all-reduce.9.cloned.1.call-start
  97.3 0.1 broadcast_in_dim.26
  97.4 0.1 div.40
  97.4 127.1 %psum.58 = f32[32]{0:T(128)S(1)} all-reduce(f32[32]{0:T(128)S(1)} %get-tuple-element.2), channel_id=1, replica_groups=mesh['samp'=64,'var'=4] {'samp'}, use_global_device_ids=true, to_apply=%region_4.5 | all-reduce | flops 32 | bytes 256 | tf_op jit(solution)/shard_map/psum | solution.py:24
  224.5 131.6 %all-reduce.7.cloned.1.call-done = f32[4096,32]{0,1:T(8,128)} async-done(((f32[4096,32]{0,1:T(8,128)}), f32[4096,32]{0,1:T(8,128)}) %all-reduce.7.cloned.1.call-update) | async-done | bytes 524304 | tf_op jit(solution)/shard_map/psum | solution.py:75
  356.1 1.8 convolution_bitcast_fusion.2
  357.9 0.5 fusion.4
  358.5 0.0 dynamic-slice-start
  358.5 14.0 %psum.60 = bf16[256,32]{0,1:T(8,128)(2,1)S(1)} all-reduce(bf16[256,32]{0,1:T(8,128)(2,1)S(1)} %fusion.4), channel_id=1, replica_groups=mesh['samp'=64,'var'=4] {'var'}, use_global_device_ids=true, to_apply=%region_7.8 | all-reduce | flops 8192 | bytes 32768 | tf_op jit(solution)/shard_map/psum | solution.py:51
  372.5 0.2 convert_reduce_fusion.1
  372.7 1.5 convolution_subtract_fusion.1
  374.2 0.0 all-reduce.9.cloned.1.call-update
  374.3 0.0 all-reduce.5.cloned.1.call-start
  374.3 4.6 fusion
  379.0 0.0 all-reduce.5.cloned.1.call-update
  379.0 0.0 all-reduce.11.cloned.1.call-start
  379.0 250.2 %all-reduce.9.cloned.1.call-done = f32[4096,32]{0,1:T(8,128)} async-done(((f32[4096,32]{0,1:T(8,128)}), f32[4096,32]{0,1:T(8,128)}) %all-reduce.9.cloned.1.call-update) | async-done | bytes 524304 | tf_op jit(solution)/shard_map/psum | solution.py:75
  629.3 1.6 multiply_add_fusion
  630.9 0.5 convolution_bitcast_fusion.1
  631.4 0.4 fusion.5
  631.9 0.0 dynamic-slice-start.1
  631.9 13.9 %psum.62 = bf16[256,32]{0,1:T(8,128)(2,1)S(1)} all-reduce(bf16[256,32]{0,1:T(8,128)(2,1)S(1)} %fusion.5), channel_id=1, replica_groups=mesh['samp'=64,'var'=4] {'var'}, use_global_device_ids=true, to_apply=%region_10.11 | all-reduce | flops 8192 | bytes 32768 | tf_op jit(solution)/shard_map/psum | solution.py:51
  645.8 0.2 convert_reduce_fusion
  646.0 1.5 convolution_subtract_fusion
  647.5 0.0 all-reduce.11.cloned.1.call-update
  647.5 172.9 %all-reduce.5.cloned.1.call-done = f32[10240,32]{0,1:T(8,128)} async-done(((f32[10240,32]{0,1:T(8,128)}), f32[10240,32]{0,1:T(8,128)}) %all-reduce.5.cloned.1.call-update) | async-done | bytes 1310736 | tf_op jit(solution)/shard_map/psum | solution.py:61
  820.4 2.3 fusion.2
  822.7 256.9 %all-reduce.11.cloned.1.call-done = f32[4096,32]{0,1:T(8,128)} async-done(((f32[4096,32]{0,1:T(8,128)}), f32[4096,32]{0,1:T(8,128)}) %all-reduce.11.cloned.1.call-update) | async-done | bytes 524304 | tf_op jit(solution)/shard_map/psum | solution.py:75
  1079.6 1.1 broadcast_multiply_fusion
  1080.6 0.8 minimum_subtract_fusion.1
  (32 shorter events, 0.1 us)
Async XLA Ops:
  7.2 348.9 %all-reduce.7.cloned.1.call-start = ((), (), s32[]{:S(2)}) async-start(), calls=%async_computation.1 | async-start | bytes 1048576 | tf_op jit(solution)/shard_map/psum | solution.py:75
  15.2 7.9 copy-start.10
  26.6 3.2 copy-start.1
  29.8 23.1 %copy-start = (f32[40960]{0:T(1024)S(1)}, f32[40960]{0:T(1024)}, u32[]{:S(2)}) copy-start(f32[40960]{0:T(1024)} %param.10) | copy-start | bytes 491524
  52.8 23.1 %copy-start.2 = (f32[4096,32]{0,1:T(8,128)S(1)}, f32[4096,32]{0,1:T(8,128)}, u32[]{:S(2)}) copy-start(f32[4096,32]{0,1:T(8,128)} %param.15) | copy-start | bytes 1572868
  79.7 15.8 %copy-start.4 = (s32[256]{0:T(256)S(1)}, s32[256]{0:T(256)}, u32[]{:S(2)}) copy-start(s32[256]{0:T(256)} %param.13) | copy-start | bytes 3076
  79.7 15.8 %copy-start.5 = (f32[256]{0:T(256)S(1)}, f32[256]{0:T(256)}, u32[]{:S(2)}) copy-start(f32[256]{0:T(256)} %param.12) | copy-start | bytes 3076
  80.1 17.1 %copy-start.9 = (f32[8]{0:T(128)S(1)}, f32[8]{0:T(128)}, u32[]{:S(2)}) copy-start(f32[8]{0:T(128)} %param.16) | copy-start | bytes 100
  80.2 144.4 %copy-start.6 = (f32[32]{0:T(128)S(1)}, f32[32]{0:T(128)}, u32[]{:S(2)}) copy-start(f32[32]{0:T(128)} %param.17) | copy-start | bytes 388
  95.7 128.9 %copy-start.7 = (f32[32]{0:T(128)}, f32[32]{0:T(128)S(1)}, u32[]{:S(2)}) copy-start(f32[32]{0:T(128)S(1)} %get-tuple-element.3) | copy-start | bytes 388
  97.2 532.1 %all-reduce.9.cloned.1.call-start = ((), (), s32[]{:S(2)}) async-start(), calls=%async_computation.2 | async-start | bytes 1048576 | tf_op jit(solution)/shard_map/psum | solution.py:75
  356.1 1.8 copy-start.3
  358.5 15.9 %dynamic-slice-start = ((f32[40960]{0:T(1024)}, s32[]{:T(128)}), f32[10240]{0:T(1024)S(1)}, s32[]{:S(2)}) async-start(f32[40960]{0:T(1024)} %param.10, s32[]{:T(128)} %select_n.39), calls=%async_computation.4 | async-start | bytes 82432 | tf_op jit(solution)/shard_map/dynamic_slice | solution.py:56
  358.5 15.9 %copy-start.8 = (f32[32]{0:T(128)S(1)}, f32[32]{0:T(128)}, u32[]{:S(2)}) copy-start(f32[32]{0:T(128)} %copy-done.7) | copy-start | bytes 388
  374.3 446.2 %all-reduce.5.cloned.1.call-start = ((), (), s32[]{:S(2)}) async-start(), calls=%async_computation | async-start | bytes 2621440 | tf_op jit(solution)/shard_map/psum | solution.py:61
  379.0 700.6 %all-reduce.11.cloned.1.call-start = ((), (), s32[]{:S(2)}) async-start(), calls=%async_computation.3 | async-start | bytes 1048576 | tf_op jit(solution)/shard_map/psum | solution.py:75
  631.9 188.6 %dynamic-slice-start.1 = ((f32[40960]{0:T(1024)}, s32[]{:T(128)}), f32[10240]{0:T(1024)S(1)}, s32[]{:S(2)}) async-start(f32[40960]{0:T(1024)} %param.11, s32[]{:T(128)} %select_n.39), calls=%async_computation.5 | async-start | bytes 82432 | tf_op jit(solution)/shard_map/dynamic_slice | solution.py:57
Sparse Core Ops, SparseCore 0:
  97.3 258.7 all-reduce.6
  374.4 254.8 all-reduce.8
  632.7 187.6 all-reduce.4
  825.7 253.7 all-reduce.10
where the time goes:
time: 1090 us
  waiting for transfers between devices  812 us (74%)
  blocking collectives  170 us (16%)
  local copies, waits for them, and re-layouts  68.7 us (6%)
  between operations  14 us (1%)
  matrix products  13.4 us (1%)
    psum x3, waiting for transfers between devices, shards(): gradient_total = lax.psum(gradient_cross, ('samp', 'var'))  639 us
    psum x1, waiting for transfers between devices, shards(): lax.psum(cross - local_centers[:, None] * column_sums[None, :], 'samp')  173 us
    psum x1, blocking collectives, shards(): counts = lax.psum(jnp.sum(weights, axis=0), 'samp')  127 us
    psum x3, blocking collectives, residual_of(): lax.psum(partial_fit.astype(jnp.bfloat16), 'var').astype(jnp.float32)  43.3 us
    gather x1, local copies, waits for them, and re-layouts, shards(): strong_scales = scales[columns]  23 us
    gather x1, local copies, waits for them, and re-layouts, shards(): strong_centers = centers[columns]  23 us
  transfers between devices with their start and end apart: 4, of which 4 were waited for; matrix products, arithmetic and copies ran while one was open for 1% of the time, Pallas kernels for 0%

commit v1 on v0

--- a/solution.py
+++ b/solution.py
@@ -1,3 +1,4 @@
+import functools
 import math
 import jax
 import jax.numpy as jnp
@@ -12,6 +13,15 @@
 exact_mode = lax.Precision.HIGHEST
 
 
+def bring_slot(sample, shard_axis):
+    side_arr = lax.all_gather(sample, shard_axis)
+    s_next = jnp.sum(side_arr, axis=0)
+    return s_next
+
+
+step_on_clusters_now = functools.partial(bring_slot, shard_axis="samp")
+
+
 def shards(
     dosage, centers, scales, phenotype, fold_ids, strong_blocks, warm_start, penalty, step_size
 ):
@@ -21,7 +31,7 @@
     fit_total = LAMBDAS * FOLDS
     fit_folds = jnp.arange(fit_total, dtype=jnp.int32) % FOLDS
     weights = (fold_ids[:, None] != fit_folds[None, :]).astype(jnp.float32)
-    counts = lax.psum(jnp.sum(weights, axis=0), "samp")
+    counts = step_on_clusters_now(jnp.sum(weights, axis=0))
     fit_penalty = jnp.repeat(penalty, FOLDS)
     threshold = step_size * fit_penalty
     local_blocks = local_width // BLOCK

time: 1090 us -> 1090 us (level)
    unnamed x0 -> x1, blocking collectives: none -> 129 us
    psum x1 -> x0, blocking collectives: 127 us -> none  [shards(): counts = lax.psum(jnp.sum(weights, axis=0), 'samp')]
where the time goes in v1:
time: 1090 us
  waiting for transfers between devices  808 us (74%)
  blocking collectives  172 us (16%)
  local copies, waits for them, and re-layouts  69.7 us (6%)
  between operations  14.8 us (1%)
  matrix products  13.4 us (1%)
    psum x3, waiting for transfers between devices, shards(): gradient_total = lax.psum(gradient_cross, ('samp', 'var'))  635 us
    psum x1, waiting for transfers between devices, shards(): lax.psum(cross - local_centers[:, None] * column_sums[None, :], 'samp')  173 us
    unnamed x1, blocking collectives  129 us
    psum x3, blocking collectives, residual_of(): lax.psum(partial_fit.astype(jnp.bfloat16), 'var').astype(jnp.float32)  43.3 us
    gather x1, local copies, waits for them, and re-layouts, shards(): strong_scales = scales[columns]  23 us
    gather x1, local copies, waits for them, and re-layouts, shards(): strong_centers = centers[columns]  23 us
  transfers between devices with their start and end apart: 4, of which 4 were waited for; matrix products, arithmetic and copies ran while one was open for 1% of the time, Pallas kernels for 0%

profile of v1, /device:TPU:2, one launch (start us, length us, event | category | flops | bytes accessed | tf_op | source)
XLA Modules:
  0.0 1087.8 jit_solution(1351358026711546876)
XLA Ops:
  7.2 0.0 all-reduce.8.cloned.1.call-start
  7.2 7.9 copy.11
  15.2 7.9 copy.12
  23.1 3.4 gather_fusion
  26.6 2.9 copy.13
  29.5 0.1 broadcast_bitcast_fusion
  29.6 0.1 broadcast_bitcast_fusion.1
  29.7 0.1 iota_add_fusion
  29.8 23.0 %gather_fusion.1 = f32[4096]{0:T(1024)S(1)} fusion(f32[40960]{0:T(1024)S(1)} %copy-done.1, s32[4096]{0:T(1024)S(1)} %broadcast_clamp_fusion), kind=kCustom, calls=%fused_computation.1 | custom fusion | bytes 49152 | tf_op jit(solution)/shard_map/gather | solution.py:48
  52.9 23.0 %gather_fusion.2 = f32[4096]{0:T(1024)S(1)} fusion(f32[40960]{0:T(1024)S(1)} %copy-done, s32[4096]{0:T(1024)S(1)} %broadcast_clamp_fusion), kind=kCustom, calls=%fused_computation.2 | custom fusion | bytes 49152 | tf_op jit(solution)/shard_map/gather | solution.py:47
  75.9 0.1 fusion.23
  76.0 0.5 convolution_bitcast_fusion.3
  76.5 3.2 fusion.1
  79.7 0.4 fusion.3
  80.2 15.3 %psum.49 = bf16[256,32]{0,1:T(8,128)(2,1)S(1)} all-reduce(bf16[256,32]{0,1:T(8,128)(2,1)S(1)} %fusion.3), channel_id=1, replica_groups=mesh['samp'=64,'var'=4] {'var'}, use_global_device_ids=true, to_apply=%region_0.1 | all-reduce | flops 8192 | bytes 32768 | tf_op jit(solution)/shard_map/psum | solution.py:61
  95.5 0.2 fusion.11
  95.7 1.5 convolution_subtract_fusion.2
  97.2 0.0 all-reduce.8.cloned.1.call-update
  97.2 0.0 all-reduce.10.cloned.1.call-start
  97.3 0.1 broadcast_in_dim.26
  97.4 0.1 div.40
  97.4 0.7 dynamic-slice
  98.8 0.3 dynamic-update-slice
  99.1 129.1 %all-reduce = f32[2048]{0:T(1024)S(1)} all-reduce(f32[2048]{0:T(1024)S(1)} %dynamic-update-slice), channel_id=2, replica_groups=mesh['samp'=64,'var'=4] {'samp'}, use_global_device_ids=true, to_apply=%add | all-reduce | flops 2048 | bytes 16384
  228.2 0.1 reshape.112
  228.4 127.6 %all-reduce.8.cloned.1.call-done = f32[4096,32]{0,1:T(8,128)} async-done(((f32[4096,32]{0,1:T(8,128)}), f32[4096,32]{0,1:T(8,128)}) %all-reduce.8.cloned.1.call-update) | async-done | bytes 524304 | tf_op jit(solution)/shard_map/psum | solution.py:85
  355.9 1.8 convolution_bitcast_fusion.2
  357.7 0.5 fusion.4
  358.3 14.0 %psum.52 = bf16[256,32]{0,1:T(8,128)(2,1)S(1)} all-reduce(bf16[256,32]{0,1:T(8,128)(2,1)S(1)} %fusion.4), channel_id=1, replica_groups=mesh['samp'=64,'var'=4] {'var'}, use_global_device_ids=true, to_apply=%region_7.8 | all-reduce | flops 8192 | bytes 32768 | tf_op jit(solution)/shard_map/psum | solution.py:61
  372.3 0.2 convert_reduce_fusion.1
  372.5 1.5 convolution_subtract_fusion.1
  374.1 0.0 all-reduce.6.cloned.1.call-start
  374.1 4.6 fusion
  378.8 0.0 all-reduce.6.cloned.1.call-update
  378.8 0.0 all-reduce.12.cloned.1.call-start
  378.9 250.3 %all-reduce.10.cloned.1.call-done = f32[4096,32]{0,1:T(8,128)} async-done(((f32[4096,32]{0,1:T(8,128)}), f32[4096,32]{0,1:T(8,128)}) %all-reduce.10.cloned.1.call-update) | async-done | bytes 524304 | tf_op jit(solution)/shard_map/psum | solution.py:85
  629.1 1.6 multiply_add_fusion
  630.7 0.5 convolution_bitcast_fusion.1
  631.2 0.4 fusion.5
  631.7 13.9 %psum.54 = bf16[256,32]{0,1:T(8,128)(2,1)S(1)} all-reduce(bf16[256,32]{0,1:T(8,128)(2,1)S(1)} %fusion.5), channel_id=1, replica_groups=mesh['samp'=64,'var'=4] {'var'}, use_global_device_ids=true, to_apply=%region_10.11 | all-reduce | flops 8192 | bytes 32768 | tf_op jit(solution)/shard_map/psum | solution.py:61
  645.6 0.2 convert_reduce_fusion
  645.8 1.5 convolution_subtract_fusion
  647.3 0.0 all-reduce.12.cloned.1.call-update
  647.3 172.9 %all-reduce.6.cloned.1.call-done = f32[10240,32]{0,1:T(8,128)} async-done(((f32[10240,32]{0,1:T(8,128)}), f32[10240,32]{0,1:T(8,128)}) %all-reduce.6.cloned.1.call-update) | async-done | bytes 1310736 | tf_op jit(solution)/shard_map/psum | solution.py:71
  820.3 2.3 fusion.2
  822.5 256.9 %all-reduce.12.cloned.1.call-done = f32[4096,32]{0,1:T(8,128)} async-done(((f32[4096,32]{0,1:T(8,128)}), f32[4096,32]{0,1:T(8,128)}) %all-reduce.12.cloned.1.call-update) | async-done | bytes 524304 | tf_op jit(solution)/shard_map/psum | solution.py:85
  1079.4 1.1 broadcast_multiply_fusion
  1080.5 0.8 minimum_subtract_fusion.1
  (39 shorter events, 0.2 us)
Async XLA Ops:
  7.2 348.8 %all-reduce.8.cloned.1.call-start = ((), (), s32[]{:S(2)}) async-start(), calls=%async_computation.1 | async-start | bytes 1048576 | tf_op jit(solution)/shard_map/psum | solution.py:85
  15.2 7.9 copy-start.10
  26.6 3.2 copy-start.1
  29.8 23.1 %copy-start = (f32[40960]{0:T(1024)S(1)}, f32[40960]{0:T(1024)}, u32[]{:S(2)}) copy-start(f32[40960]{0:T(1024)} %param.10) | copy-start | bytes 491524
  52.8 23.1 %copy-start.2 = (f32[4096,32]{0,1:T(8,128)S(1)}, f32[4096,32]{0,1:T(8,128)}, u32[]{:S(2)}) copy-start(f32[4096,32]{0,1:T(8,128)} %param.15) | copy-start | bytes 1572868
  79.7 15.8 %copy-start.4 = (s32[256]{0:T(256)S(1)}, s32[256]{0:T(256)}, u32[]{:S(2)}) copy-start(s32[256]{0:T(256)} %param.13) | copy-start | bytes 3076
  79.7 15.8 %copy-start.5 = (f32[256]{0:T(256)S(1)}, f32[256]{0:T(256)}, u32[]{:S(2)}) copy-start(f32[256]{0:T(256)} %param.12) | copy-start | bytes 3076
  80.1 17.1 %copy-start.9 = (f32[8]{0:T(128)S(1)}, f32[8]{0:T(128)}, u32[]{:S(2)}) copy-start(f32[8]{0:T(128)} %param.16) | copy-start | bytes 100
  80.2 17.3 %copy-start.11 = (u32[256]{0:T(256)S(1)}, u32[256]{0:T(256)}, u32[]{:S(2)}) copy-start(u32[256]{0:T(256)} %constant.64) | copy-start | bytes 3076
  80.2 148.2 %copy-start.6 = (f32[32]{0:T(128)S(1)}, f32[32]{0:T(128)}, u32[]{:S(2)}) copy-start(f32[32]{0:T(128)} %param.17) | copy-start | bytes 388
  95.7 132.7 %copy-start.7 = (f32[32]{0:T(128)}, f32[32]{0:T(128)S(1)}, u32[]{:S(2)}) copy-start(f32[32]{0:T(128)S(1)} %get-tuple-element.3) | copy-start | bytes 388
  97.2 531.9 %all-reduce.10.cloned.1.call-start = ((), (), s32[]{:S(2)}) async-start(), calls=%async_computation.2 | async-start | bytes 1048576 | tf_op jit(solution)/shard_map/psum | solution.py:85
  355.9 1.8 copy-start.3
  358.3 15.9 %dynamic-slice-start = ((f32[40960]{0:T(1024)}, s32[]{:T(128)}), f32[10240]{0:T(1024)S(1)}, s32[]{:S(2)}) async-start(f32[40960]{0:T(1024)} %param.10, s32[]{:T(128)} %select_n.39), calls=%async_computation.4 | async-start | bytes 82432 | tf_op jit(solution)/shard_map/dynamic_slice | solution.py:66
  358.3 15.9 %copy-start.8 = (f32[32]{0:T(128)S(1)}, f32[32]{0:T(128)}, u32[]{:S(2)}) copy-start(f32[32]{0:T(128)} %copy-done.7) | copy-start | bytes 388
  374.1 446.2 %all-reduce.6.cloned.1.call-start = ((), (), s32[]{:S(2)}) async-start(), calls=%async_computation | async-start | bytes 2621440 | tf_op jit(solution)/shard_map/psum | solution.py:71
  378.8 700.6 %all-reduce.12.cloned.1.call-start = ((), (), s32[]{:S(2)}) async-start(), calls=%async_computation.3 | async-start | bytes 1048576 | tf_op jit(solution)/shard_map/psum | solution.py:85
  631.7 188.6 %dynamic-slice-start.1 = ((f32[40960]{0:T(1024)}, s32[]{:T(128)}), f32[10240]{0:T(1024)S(1)}, s32[]{:S(2)}) async-start(f32[40960]{0:T(1024)} %param.11, s32[]{:T(128)} %select_n.39), calls=%async_computation.5 | async-start | bytes 82432 | tf_op jit(solution)/shard_map/dynamic_slice | solution.py:67
Sparse Core Ops, SparseCore 0:
  97.3 258.5 all-reduce.7
  374.2 254.8 all-reduce.9
  632.6 187.6 all-reduce.5
  825.6 253.7 all-reduce.11
